TPU v7x, 128 devices: a whole 4x4x4 slice. The times are simulated.
128 devices in a mesh: row: 16 (over x, y), col: 8 (over z, core).
Axes of the slice: x: 4, y: 4, z: 4, core: 2. Of those that a mesh axis runs over, the one named last changes fastest.
Arguments:
- orbitals: bfloat16 [131072, 512], P(('row', 'col')), may hold values from -6 to 6
- coulomb: bfloat16 [32768, 32768], P('row', 'col'), may hold values from -0.0014648438 to 0.0014648438
- interp: bfloat16 [131072, 1024], P(('row', 'col')), may hold values from -0.1875 to 0.1875
- box_counts: int32 [128], replicated, may hold values from 1 to 768, 32768 in all
- owner_map: int32 [32768], replicated, may hold values from 0 to 32767, as said below
- grid_rows: int32 [128, 1024], P(('row', 'col')), may hold values from 0 to 1023, each once within a row
- listed: int32 [128, 1024], P(('row', 'col')), may hold values from 0 to 255
Outputs:
- exchange_action: float32 [131072, 512], P(('row', 'col'))
Inputs may be any that keep to these rules, and one draw needn't show every extreme that they name: `box_counts`: the counts sum to 32768; the largest is exactly 768. `owner_map`: A permutation of the 32768 positions; a point's owner is position // 256. No box holds more than 6 points of one owner, and the box with 768 points holds exactly 6 of some owner. `grid_rows`: each row is a permutation.
All inputs are finite; a program needn't handle non-finite values.
Results may differ from a plain program's by a relative error of at most 0.012.
Values may be sent and summed in bfloat16 or wider, within the bound.
A program may use at most 128 MiB of HBM per device.

v0:
```python
import jax
import jax.numpy as jnp
from jax import lax
from jax.sharding import PartitionSpec as P

NORB = 512
LIST = 1024
OWN = 256
SLOTS = 768


def copy_for_each(x, axis):
    copies = jnp.broadcast_to(x, (lax.axis_size(axis), *x.shape))
    return lax.all_to_all(copies, axis, split_axis=0, concat_axis=0, tiled=True)


def in_order(parts, dim):
    parts = jnp.moveaxis(parts, 0, dim)
    dims = parts.shape
    return parts.reshape(*dims[:dim], dims[dim] * dims[dim + 1], *dims[dim + 2 :])


def gather_directly(x, axis, dim):
    parts = copy_for_each(x, axis)
    return in_order(parts, dim)


def add_block(shard_rows, left_rows, kernel_tile):
    pair_tile = jnp.einsum(
        "ak,bk->ab", left_rows, shard_rows, preferred_element_type=jnp.float32
    ).astype(jnp.bfloat16)
    weighted = (pair_tile.astype(jnp.float32) * kernel_tile.astype(jnp.float32)).astype(
        jnp.bfloat16
    )
    return jnp.dot(weighted, shard_rows, preferred_element_type=jnp.float32)


def shards(orbitals, coulomb, interp, box_counts, owner_map, grid_rows, listed):
    row_count = lax.axis_size("row")
    col_count = lax.axis_size("col")
    box_total = row_count * col_count
    point_total = OWN * box_total
    capacity = (SLOTS + box_total - 1) // box_total
    per_owner = LIST // box_total
    my_box = lax.axis_index("row") * col_count + lax.axis_index("col")
    box_ids = jnp.arange(box_total, dtype=jnp.int32)
    first_point = jnp.sum(jnp.where(box_ids < my_box, box_counts, 0))
    my_count = jnp.sum(jnp.where(box_ids == my_box, box_counts, 0))
    slot_ids = jnp.arange(SLOTS, dtype=jnp.int32)
    is_live = slot_ids < my_count
    listing = jnp.minimum(first_point + slot_ids, point_total - 1)
    owner_ids = owner_map[listing] // OWN
    matches = (
        (owner_ids[:, None] == owner_ids[None, :])
        & is_live[None, :]
        & (slot_ids[None, :] < slot_ids[:, None])
    )
    pair_rank = jnp.sum(matches.astype(jnp.int32), axis=1)
    target = jnp.where(is_live, owner_ids * capacity + pair_rank, box_total * capacity)
    dest_slots = jnp.arange(box_total * capacity, dtype=jnp.int32)
    hits = target[None, :] == dest_slots[:, None]
    source_slot = jnp.sum(jnp.where(hits, slot_ids[None, :], 0), axis=1)
    filled = jnp.any(hits, axis=1)
    picked = orbitals[grid_rows[0, source_slot]]
    outgoing = jnp.where(filled[:, None], picked, jnp.zeros_like(picked))
    received = lax.all_to_all(
        outgoing.reshape(box_total, capacity, NORB),
        ("row", "col"),
        split_axis=0,
        concat_axis=0,
        tiled=True,
    )
    received = received.reshape(box_total * capacity, NORB)
    wanted_pos = my_box * OWN + jnp.arange(OWN, dtype=jnp.int32)
    all_listing = jnp.arange(point_total, dtype=jnp.int32)
    my_points = jnp.sum(
        jnp.where(owner_map[None, :] == wanted_pos[:, None], all_listing[None, :], 0), axis=1
    )
    box_ends = jnp.cumsum(box_counts)
    source = jnp.sum((my_points[:, None] >= box_ends[None, :]).astype(jnp.int32), axis=1)
    earlier = (source[:, None] == source[None, :]) & (my_points[None, :] < my_points[:, None])
    source_rank = jnp.sum(earlier.astype(jnp.int32), axis=1)
    owned_rows = received[source * capacity + source_rank]
    left_rows = gather_directly(owned_rows, "col", 0)
    partial_sums = add_block(
        lax.all_gather(owned_rows, "row", axis=0, tiled=True), left_rows, coulomb
    )
    owned_result = lax.psum_scatter(partial_sums, "col", scatter_dimension=0, tiled=True).astype(
        jnp.bfloat16
    )
    wanted = listed[0].reshape(box_total, per_owner)
    fetched = lax.all_to_all(
        owned_result[
            lax.all_to_all(wanted, ("row", "col"), split_axis=0, concat_axis=0, tiled=True)
        ],
        ("row", "col"),
        split_axis=0,
        concat_axis=0,
        tiled=True,
    )
    chosen_rows = fetched.reshape(LIST, NORB)
    return -jnp.dot(interp, chosen_rows, preferred_element_type=jnp.float32)


def solution(mesh):
    return jax.shard_map(
        shards,
        mesh=mesh,
        in_specs=(
            P(("row", "col"), None),
            P("row", "col"),
            P(("row", "col"), None),
            P(),
            P(),
            P(("row", "col"), None),
            P(("row", "col"), None),
        ),
        out_specs=P(("row", "col"), None),
        check_vma=False,
    )
```

profile of v0, /device:TPU:1, one launch (start us, length us, event | category | flops | bytes accessed | tf_op | source)
XLA Modules:
  0.0 216.9 jit_solution(2038270782259860773)
XLA Ops:
  6.5 0.0 copy-start
  6.5 1.5 fusion.12
  8.1 0.7 fusion.7
  8.8 4.7 %gather_fusion = s32[768]{0:T(1024)S(1)} fusion(s32[32768]{0:T(1024)} %param.11, s32[1024]{0:T(1024)S(1)} %pad_clamp_fusion.2), kind=kCustom, calls=%fused_computation | custom fusion | bytes 9216 | tf_op jit(solution)/shard_map/gather | solution.py:52
  13.5 0.0 copy-start.3
  13.5 0.7 iota_compare_fusion.2
  14.2 0.4 convert_reduce_fusion
  14.7 0.7 add_select_fusion.1
  15.3 0.3 select_reduce_fusion.1
  15.6 0.3 fusion.2
  16.0 4.7 %gather_fusion.1 = s32[768]{0:T(1024)S(1)} fusion(s32[1,1024]{1,0:T(1,128)S(1)} %copy-done.1, s32[768]{0:T(1024)S(1)} %fusion.11), kind=kCustom, calls=%fused_computation.1 | custom fusion | bytes 12288 | tf_op jit(solution)/shard_map/gather | solution.py:64
  20.7 3.3 %gather_fusion.2 = bf16[768,512]{1,0:T(8,128)(2,1)} fusion(bf16[1024,512]{1,0:T(8,128)(2,1)S(1)} %copy-done.3, s32[1024]{0:T(1024)S(1)} %pad_clamp_fusion.1), kind=kCustom, calls=%fused_computation.2 | custom fusion | bytes 1575936 | tf_op jit(solution)/shard_map/gather | solution.py:64
  24.1 1.3 gather.23
  25.4 0.0 copy-start.2
  25.4 0.0 copy-start.5
  25.4 0.2 broadcast_in_dim.47
  25.6 1.2 broadcast_select_fusion
  26.8 12.0 %all-to-all-start = ((bf16[128,6,512]{2,1,0:T(8,128)(2,1)}), bf16[128,6,512]{2,1,0:T(8,128)(2,1)}, u32[]{:S(2)}, u32[]{:S(2)}) async-start(bf16[128,6,512]{2,1,0:T(8,128)(2,1)} %broadcast_select_fusion), calls=%async_computation | async-start | bytes 2097152 | tf_op jit(solution)/shard_map/all_to_all | solution.py:66
  38.7 0.0 all-gather.3.cloned.1.call-start
  38.8 4.6 %select_reduce_fusion = s32[256]{0:T(256)S(1)} fusion(s32[32768]{0:T(1024)S(1)} %copy-done.2, s32[256]{0:T(256)S(1)} %iota_add_fusion), kind=kLoop, calls=%fused_computation.6 | loop fusion | flops 25165568 | bytes 133120 | tf_op jit(solution)/shard_map/reduce_sum | solution.py:76
  43.4 0.0 copy-done.5
  43.4 0.1 copy.15
  43.5 0.2 reduce-window.8
  43.7 0.1 reduce.3
  43.8 0.2 convert_reduce_fusion.2
  44.0 0.2 convert_reduce_fusion.1
  44.3 13.4 %all-to-all-done = bf16[128,6,512]{2,1,0:T(8,128)(2,1)} async-done(((bf16[128,6,512]{2,1,0:T(8,128)(2,1)}), bf16[128,6,512]{2,1,0:T(8,128)(2,1)}, u32[]{:S(2)}, u32[]{:S(2)}) %all-to-all-start) | async-done | bytes 786464 | tf_op jit(solution)/shard_map/all_to_all | solution.py:66
  57.7 1.4 reshape.199
  59.0 1.9 gather_fusion.3
  60.9 0.0 all-gather.3.cloned.1.call-update
  60.9 0.0 reduce-scatter.2.cloned.1.call-start
  61.0 1.1 broadcast_in_dim.79
  62.1 30.8 %all_to_all.27 = bf16[8,256,512]{2,1,0:T(8,128)(2,1)} all-to-all(bf16[8,256,512]{2,1,0:T(8,128)(2,1)S(1)} %broadcast_in_dim.79), channel_id=1, replica_groups=mesh['row'=16,'col'=8] {'col'}, dimensions={0} | all-to-all | bytes 4194304 | tf_op jit(solution)/shard_map/all_to_all | solution.py:14
  92.9 15.8 %all-gather.3.cloned.1.call-done = bf16[4096,512]{1,0:T(8,128)(2,1)} async-done(((bf16[256,512]{1,0:T(8,128)(2,1)}), bf16[4096,512]{1,0:T(8,128)(2,1)}) %all-gather.3.cloned.1.call-update) | async-done | bytes 4194320 | tf_op jit(solution)/shard_map/all_gather | solution.py:86
  108.7 26.1 %fusion = f32[2048,512]{1,0:T(8,128)} fusion(bf16[4096,512]{1,0:T(8,128)(2,1)} %all-gather.3.cloned.1.call-done, bf16[2048,4096]{1,0:T(8,128)(2,1)} %param.8, bf16[2048,512]{1,0:T(8,128)(2,1)} %bitcast.27), kind=kOutput, calls=%fused_computation.7 | convolution fusion | flops 17213423616 | bytes 27262976 | tf_op jit(solution)/shard_map/dot_general | solution.py:35
  134.8 0.0 reduce-scatter.2.cloned.1.call-update
  134.8 0.5 broadcast.260
  135.3 0.1 copy-done.4
  135.5 0.7 reduce.10
  136.1 0.1 all_to_all.19
  136.2 17.2 %all_to_all.28 = s32[128,1,8]{2,1,0:T(1,128)S(1)} all-to-all(s32[128,1,8]{2,1,0:T(1,128)S(1)} %bitcast.28), channel_id=1, replica_groups=mesh['row'=16,'col'=8] {'row','col'}, dimensions={0} | all-to-all | bytes 8192 | tf_op jit(solution)/shard_map/all_to_all | solution.py:94
  153.4 0.1 reshape.236
  153.5 16.8 %reduce-scatter.2.cloned.1.call-done = f32[256,512]{1,0:T(8,128)} async-done(((f32[2048,512]{1,0:T(8,128)}), f32[256,512]{1,0:T(8,128)}) %reduce-scatter.2.cloned.1.call-update) | async-done | bytes 524304 | tf_op jit(solution)/shard_map/reduce_scatter | solution.py:88
  170.3 1.1 convert_element_type.31
  171.4 4.0 %gather_fusion.4 = bf16[1024,512]{1,0:T(8,128)(2,1)S(1)} fusion(bf16[256,512]{1,0:T(8,128)(2,1)S(1)} %convert_element_type.31, s32[1024]{0:T(1024)S(1)} %broadcast_clamp_fusion), kind=kCustom, calls=%fused_computation.4 | custom fusion | bytes 2101248 | tf_op jit(solution)/shard_map/gather | solution.py:93
  175.4 29.2 %all_to_all.29 = bf16[128,8,512]{2,1,0:T(8,128)(2,1)S(1)} all-to-all(bf16[128,8,512]{2,1,0:T(8,128)(2,1)S(1)} %bitcast.26), channel_id=1, replica_groups=mesh['row'=16,'col'=8] {'row','col'}, dimensions={0} | all-to-all | bytes 2097152 | tf_op jit(solution)/shard_map/all_to_all | solution.py:92
  204.5 2.6 %negate_bitcast_fusion = f32[1024,512]{0,1:T(8,128)} fusion(bf16[1024,1024]{1,0:T(8,128)(2,1)S(1)} %copy-done, bf16[128,8,512]{2,1,0:T(8,128)(2,1)S(1)} %all_to_all.29), kind=kOutput, calls=%fused_computation.15 | convolution fusion | flops 1074266112 | bytes 5242880 | tf_op jit(solution)/shard_map/dot_general | solution.py:102
  207.2 2.9 %copy.17 = f32[1024,512]{1,0:T(8,128)} copy(f32[1024,512]{0,1:T(8,128)} %negate_bitcast_fusion) | data formatting | bytes 4194304 | tf_op jit(solution)/shard_map/neg | solution.py:102
  (17 shorter events, 0.1 us)
Async XLA Ops:
  6.5 198.0 %copy-start = (bf16[1024,1024]{1,0:T(8,128)(2,1)S(1)}, bf16[1024,1024]{1,0:T(8,128)(2,1)}, u32[]{:S(2)}) copy-start(bf16[1024,1024]{1,0:T(8,128)(2,1)} %param.9) | copy-start | bytes 6291460
  6.5 9.5 %copy-start.1 = (s32[1,1024]{1,0:T(1,128)S(1)}, s32[1,1024]{1,0:T(1,128)}, u32[]{:S(2)}) copy-start(s32[1,1024]{1,0:T(1,128)} %param.12) | copy-start | bytes 12292
  13.5 7.3 %copy-start.3 = (bf16[1024,512]{1,0:T(8,128)(2,1)S(1)}, bf16[1024,512]{1,0:T(8,128)(2,1)}, u32[]{:S(2)}) copy-start(bf16[1024,512]{1,0:T(8,128)(2,1)} %param.7) | copy-start | bytes 3145732
  25.4 13.4 %copy-start.2 = (s32[32768]{0:T(1024)S(1)}, s32[32768]{0:T(1024)}, u32[]{:S(2)}) copy-start(s32[32768]{0:T(1024)} %param.11) | copy-start | bytes 393220
  25.4 18.0 %copy-start.5 = (s32[128]{0:T(128)S(1)}, s32[128]{0:T(128)}, u32[]{:S(2)}) copy-start(s32[128]{0:T(128)} %param.10) | copy-start | bytes 1540
  26.8 30.9 %all-to-all-start = ((bf16[128,6,512]{2,1,0:T(8,128)(2,1)}), bf16[128,6,512]{2,1,0:T(8,128)(2,1)}, u32[]{:S(2)}, u32[]{:S(2)}) async-start(bf16[128,6,512]{2,1,0:T(8,128)(2,1)} %broadcast_select_fusion), calls=%async_computation | async-start | bytes 2097152 | tf_op jit(solution)/shard_map/all_to_all | solution.py:66
  38.7 70.0 %all-gather.3.cloned.1.call-start = ((), (), s32[]{:S(2)}) async-start(), calls=%async_computation.6 | async-start | bytes 4456448 | tf_op jit(solution)/shard_map/all_gather | solution.py:86
  60.9 109.4 %reduce-scatter.2.cloned.1.call-start = ((), (), s32[]{:S(2)}) async-start(), calls=%async_computation.5 | async-start | bytes 4718592 | tf_op jit(solution)/shard_map/reduce_scatter | solution.py:88
  134.8 0.7 copy-start.4
Sparse Core Ops, SparseCore 0:
  61.0 47.5 all-gather.2
  134.9 35.3 reduce-scatter.1
where the time goes:
time: 217 us
  blocking collectives  77.1 us (36%)
  waiting for transfers between devices  46 us (21%)
  matrix products  28.8 us (13%)
  local copies, waits for them, and re-layouts  26.3 us (12%)
  between operations  13.7 us (6%)
  other arithmetic  13 us (6%)
  starting transfers between devices  12 us (6%)
    all_to_all x1, blocking collectives, copy_for_each(): return lax.all_to_all(copies, axis, split_axis=0, concat_axis=0, tiled=True)  30.8 us
    all_to_all x1, blocking collectives, shards(): lax.all_to_all(owned_result[lax.all_to_all(wanted, ('row', 'col'), split_...  29.2 us
    dot_general x1, matrix products, add_block(): return jnp.dot(weighted, shard_rows, preferred_element_type=jnp.float32)  26.1 us
    all_to_all x1, blocking collectives, shards(): lax.all_to_all(wanted, ('row', 'col'), split_axis=0, concat_axis=0, tiled...  17.2 us
    reduce_scatter x1, waiting for transfers between devices, shards(): lax.psum_scatter(partial_sums, 'col', scatter_dimension=0, tiled=True)  16.8 us
    all_gather x1, waiting for transfers between devices, shards(): lax.all_gather(owned_rows, 'row', axis=0, tiled=True)  15.8 us
    all_to_all x1, waiting for transfers between devices, shards(): lax.all_to_all(outgoing.reshape(box_total, capacity, NORB), ('row', 'col'...  13.4 us
    all_to_all x1, starting transfers between devices, shards(): lax.all_to_all(outgoing.reshape(box_total, capacity, NORB), ('row', 'col'...  12 us
  transfers between devices with their start and end apart: 3, of which 3 were waited for; matrix products, arithmetic and copies ran while one was open for 4% of the time, Pallas kernels for 0%

commit v1 on v0

--- a/solution.py
+++ b/solution.py
@@ -83,7 +83,11 @@
     owned_rows = received[source * capacity + source_rank]
     left_rows = gather_directly(owned_rows, "col", 0)
     partial_sums = add_block(
-        lax.all_gather(owned_rows, "row", axis=0, tiled=True), left_rows, coulomb
+        jnp.concatenate(
+            lax.all_to_all(jnp.stack([owned_rows] * lax.axis_size("row")), "row", 0, 0), axis=0
+        ),
+        left_rows,
+        coulomb,
     )
     owned_result = lax.psum_scatter(partial_sums, "col", scatter_dimension=0, tiled=True).astype(
         jnp.bfloat16

time: 217 us -> 252 us (1.16)
  blocking collectives: 77.1 us -> 129 us
  waiting for transfers between devices: 46 us -> 30.2 us
    all_to_all x0 -> x1, blocking collectives: none -> 52.4 us  [shards(): lax.all_to_all(jnp.stack([owned_rows] * lax.axis_size('row')), 'row', 0, 0)]
    all_gather x1 -> x0, waiting for transfers between devices: 15.8 us -> none  [shards(): lax.all_gather(owned_rows, 'row', axis=0, tiled=True)]
  transfers between devices with their start and end apart: 3 -> 2, of which waited for: 3 -> 2; matrix products, arithmetic and copies ran while one was open for 4% -> 3% of each run, Pallas kernels for 0% -> 0%
where the time goes in v1:
time: 252 us; the launch traced here: 251 us
  blocking collectives  129 us (51%)
  waiting for transfers between devices  30.2 us (12%)
  matrix products  28.8 us (11%)
  local copies, waits for them, and re-layouts  25.1 us (10%)
  between operations  13.7 us (5%)
  other arithmetic  13 us (5%)
  starting transfers between devices  12 us (5%)
    all_to_all x1, blocking collectives, shards(): lax.all_to_all(jnp.stack([owned_rows] * lax.axis_size('row')), 'row', 0, 0)  52.4 us
    all_to_all x1, blocking collectives, copy_for_each(): return lax.all_to_all(copies, axis, split_axis=0, concat_axis=0, tiled=True)  30.8 us
    all_to_all x1, blocking collectives, shards(): lax.all_to_all(owned_result[lax.all_to_all(wanted, ('row', 'col'), split_...  29.3 us
    dot_general x1, matrix products, add_block(): return jnp.dot(weighted, shard_rows, preferred_element_type=jnp.float32)  26.1 us
    reduce_scatter x1, waiting for transfers between devices, shards(): lax.psum_scatter(partial_sums, 'col', scatter_dimension=0, tiled=True)  16.8 us
    all_to_all x1, blocking collectives, shards(): lax.all_to_all(wanted, ('row', 'col'), split_axis=0, concat_axis=0, tiled...  16 us
    all_to_all x1, waiting for transfers between devices, shards(): lax.all_to_all(outgoing.reshape(box_total, capacity, NORB), ('row', 'col'...  13.4 us
    all_to_all x1, starting transfers between devices, shards(): lax.all_to_all(outgoing.reshape(box_total, capacity, NORB), ('row', 'col'...  12 us
  transfers between devices with their start and end apart: 2, of which 2 were waited for; matrix products, arithmetic and copies ran while one was open for 3% of the time, Pallas kernels for 0%

profile of v1, /device:TPU:1, one launch (start us, length us, event | category | flops | bytes accessed | tf_op | source)
XLA Modules:
  0.0 251.2 jit_solution(15834934665047214651)
XLA Ops:
  6.5 0.0 copy-start
  6.5 1.5 fusion.12
  8.1 0.7 fusion.7
  8.8 4.7 %gather_fusion = s32[768]{0:T(1024)S(1)} fusion(s32[32768]{0:T(1024)} %param.11, s32[1024]{0:T(1024)S(1)} %pad_clamp_fusion.2), kind=kCustom, calls=%fused_computation | custom fusion | bytes 9216 | tf_op jit(solution)/shard_map/gather | solution.py:52
  13.5 0.0 copy-start.3
  13.5 0.7 iota_compare_fusion.2
  14.2 0.4 convert_reduce_fusion
  14.7 0.7 add_select_fusion.1
  15.3 0.3 select_reduce_fusion.1
  15.6 0.3 fusion.2
  16.0 4.7 %gather_fusion.1 = s32[768]{0:T(1024)S(1)} fusion(s32[1,1024]{1,0:T(1,128)S(1)} %copy-done.1, s32[768]{0:T(1024)S(1)} %fusion.11), kind=kCustom, calls=%fused_computation.1 | custom fusion | bytes 12288 | tf_op jit(solution)/shard_map/gather | solution.py:64
  20.7 3.3 %gather_fusion.2 = bf16[768,512]{1,0:T(8,128)(2,1)} fusion(bf16[1024,512]{1,0:T(8,128)(2,1)S(1)} %copy-done.3, s32[1024]{0:T(1024)S(1)} %pad_clamp_fusion.1), kind=kCustom, calls=%fused_computation.2 | custom fusion | bytes 1575936 | tf_op jit(solution)/shard_map/gather | solution.py:64
  24.1 1.3 gather.23
  25.4 0.0 copy-start.2
  25.4 0.0 copy-start.5
  25.4 0.2 broadcast_in_dim.47
  25.6 1.2 broadcast_select_fusion
  26.8 12.0 %all-to-all-start = ((bf16[128,6,512]{2,1,0:T(8,128)(2,1)}), bf16[128,6,512]{2,1,0:T(8,128)(2,1)}, u32[]{:S(2)}, u32[]{:S(2)}) async-start(bf16[128,6,512]{2,1,0:T(8,128)(2,1)} %broadcast_select_fusion), calls=%async_computation | async-start | bytes 2097152 | tf_op jit(solution)/shard_map/all_to_all | solution.py:66
  38.7 0.0 reduce-scatter.2.cloned.1.call-start
  38.8 4.6 %select_reduce_fusion = s32[256]{0:T(256)S(1)} fusion(s32[32768]{0:T(1024)S(1)} %copy-done.2, s32[256]{0:T(256)S(1)} %iota_add_fusion), kind=kLoop, calls=%fused_computation.6 | loop fusion | flops 25165568 | bytes 133120 | tf_op jit(solution)/shard_map/reduce_sum | solution.py:76
  43.4 0.0 copy-done.5
  43.4 0.1 copy.15
  43.5 0.2 reduce-window.8
  43.7 0.1 reduce.3
  43.8 0.2 convert_reduce_fusion.2
  44.0 0.2 convert_reduce_fusion.1
  44.3 13.4 %all-to-all-done = bf16[128,6,512]{2,1,0:T(8,128)(2,1)} async-done(((bf16[128,6,512]{2,1,0:T(8,128)(2,1)}), bf16[128,6,512]{2,1,0:T(8,128)(2,1)}, u32[]{:S(2)}, u32[]{:S(2)}) %all-to-all-start) | async-done | bytes 786464 | tf_op jit(solution)/shard_map/all_to_all | solution.py:66
  57.7 1.4 reshape.204
  59.0 1.2 gather_fusion.3
  60.2 0.2 broadcast_in_dim.79
  60.4 30.8 %all_to_all.32 = bf16[8,256,512]{2,1,0:T(8,128)(2,1)} all-to-all(bf16[8,256,512]{2,1,0:T(8,128)(2,1)S(1)} %broadcast_in_dim.79), channel_id=1, replica_groups=mesh['row'=16,'col'=8] {'col'}, dimensions={0} | all-to-all | bytes 4194304 | tf_op jit(solution)/shard_map/all_to_all | solution.py:14
  91.2 0.4 stack.2
  91.6 52.4 %all_to_all.33 = bf16[16,256,512]{2,1,0:T(8,128)(2,1)} all-to-all(bf16[16,256,512]{2,1,0:T(8,128)(2,1)S(1)} %stack.2), channel_id=1, replica_groups=mesh['row'=16,'col'=8] {'row'}, dimensions={0} | all-to-all | bytes 8388608 | tf_op jit(solution)/shard_map/all_to_all | solution.py:87
  144.0 26.1 %fusion = f32[2048,512]{1,0:T(8,128)} fusion(bf16[4096,512]{1,0:T(8,128)(2,1)} %bitcast.28, bf16[2048,4096]{1,0:T(8,128)(2,1)} %param.8, bf16[2048,512]{1,0:T(8,128)(2,1)} %bitcast.29), kind=kOutput, calls=%fused_computation.7 | convolution fusion | flops 17213423616 | bytes 27262976 | tf_op jit(solution)/shard_map/dot_general | solution.py:35
  170.1 0.0 reduce-scatter.2.cloned.1.call-update
  170.1 0.5 broadcast.262
  170.7 0.1 copy-done.4
  170.8 0.7 reduce.10
  171.5 0.1 all_to_all.23
  171.6 16.0 %all_to_all.34 = s32[128,1,8]{2,1,0:T(1,128)S(1)} all-to-all(s32[128,1,8]{2,1,0:T(1,128)S(1)} %bitcast.30), channel_id=1, replica_groups=mesh['row'=16,'col'=8] {'row','col'}, dimensions={0} | all-to-all | bytes 8192 | tf_op jit(solution)/shard_map/all_to_all | solution.py:98
  187.6 0.1 reshape.242
  187.7 16.8 %reduce-scatter.2.cloned.1.call-done = f32[256,512]{1,0:T(8,128)} async-done(((f32[2048,512]{1,0:T(8,128)}), f32[256,512]{1,0:T(8,128)}) %reduce-scatter.2.cloned.1.call-update) | async-done | bytes 524304 | tf_op jit(solution)/shard_map/reduce_scatter | solution.py:92
  204.5 1.1 convert_element_type.31
  205.6 4.0 %gather_fusion.4 = bf16[1024,512]{1,0:T(8,128)(2,1)S(1)} fusion(bf16[256,512]{1,0:T(8,128)(2,1)S(1)} %convert_element_type.31, s32[1024]{0:T(1024)S(1)} %broadcast_clamp_fusion), kind=kCustom, calls=%fused_computation.4 | custom fusion | bytes 2101248 | tf_op jit(solution)/shard_map/gather | solution.py:97
  209.6 29.3 %all_to_all.35 = bf16[128,8,512]{2,1,0:T(8,128)(2,1)S(1)} all-to-all(bf16[128,8,512]{2,1,0:T(8,128)(2,1)S(1)} %bitcast.27), channel_id=1, replica_groups=mesh['row'=16,'col'=8] {'row','col'}, dimensions={0} | all-to-all | bytes 2097152 | tf_op jit(solution)/shard_map/all_to_all | solution.py:96
  238.9 0.0 copy-done
  238.9 2.7 %negate_bitcast_fusion = f32[1024,512]{0,1:T(8,128)} fusion(bf16[1024,1024]{1,0:T(8,128)(2,1)S(1)} %copy-done, bf16[128,8,512]{2,1,0:T(8,128)(2,1)S(1)} %all_to_all.35), kind=kOutput, calls=%fused_computation.15 | convolution fusion | flops 1074266112 | bytes 5242880 | tf_op jit(solution)/shard_map/dot_general | solution.py:106
  241.5 2.9 %copy.17 = f32[1024,512]{1,0:T(8,128)} copy(f32[1024,512]{0,1:T(8,128)} %negate_bitcast_fusion) | data formatting | bytes 4194304 | tf_op jit(solution)/shard_map/neg | solution.py:106
  (16 shorter events, 0.1 us)
Async XLA Ops:
  6.5 232.3 %copy-start = (bf16[1024,1024]{1,0:T(8,128)(2,1)S(1)}, bf16[1024,1024]{1,0:T(8,128)(2,1)}, u32[]{:S(2)}) copy-start(bf16[1024,1024]{1,0:T(8,128)(2,1)} %param.9) | copy-start | bytes 6291460
  6.5 9.5 %copy-start.1 = (s32[1,1024]{1,0:T(1,128)S(1)}, s32[1,1024]{1,0:T(1,128)}, u32[]{:S(2)}) copy-start(s32[1,1024]{1,0:T(1,128)} %param.12) | copy-start | bytes 12292
  13.5 7.3 %copy-start.3 = (bf16[1024,512]{1,0:T(8,128)(2,1)S(1)}, bf16[1024,512]{1,0:T(8,128)(2,1)}, u32[]{:S(2)}) copy-start(bf16[1024,512]{1,0:T(8,128)(2,1)} %param.7) | copy-start | bytes 3145732
  25.4 13.4 %copy-start.2 = (s32[32768]{0:T(1024)S(1)}, s32[32768]{0:T(1024)}, u32[]{:S(2)}) copy-start(s32[32768]{0:T(1024)} %param.11) | copy-start | bytes 393220
  25.4 18.0 %copy-start.5 = (s32[128]{0:T(128)S(1)}, s32[128]{0:T(128)}, u32[]{:S(2)}) copy-start(s32[128]{0:T(128)} %param.10) | copy-start | bytes 1540
  26.8 30.9 %all-to-all-start = ((bf16[128,6,512]{2,1,0:T(8,128)(2,1)}), bf16[128,6,512]{2,1,0:T(8,128)(2,1)}, u32[]{:S(2)}, u32[]{:S(2)}) async-start(bf16[128,6,512]{2,1,0:T(8,128)(2,1)} %broadcast_select_fusion), calls=%async_computation | async-start | bytes 2097152 | tf_op jit(solution)/shard_map/all_to_all | solution.py:66
  38.7 165.8 %reduce-scatter.2.cloned.1.call-start = ((), (), s32[]{:S(2)}) async-start(), calls=%async_computation.6 | async-start | bytes 4718592 | tf_op jit(solution)/shard_map/reduce_scatter | solution.py:92
  170.1 0.7 copy-start.4
Sparse Core Ops, SparseCore 0:
  170.3 34.2 reduce-scatter.1
